TPU v7x, 128 devices: a whole 4x4x4 slice. The times are simulated.
128 devices in a mesh: expert: 8 (over z, core), fsdp: 16 (over y, x).
Axes of the slice: x: 4, y: 4, z: 4, core: 2. Of those that a mesh axis runs over, the one named last changes fastest.
Arguments:
- tokens: bfloat16 [32768, 2048], P(('expert', 'fsdp')), may hold values from -6 to 6
- expert_ids: int32 [32768, 6], P(('expert', 'fsdp')), may hold values from 0 to 63, as said below
- gate_vals: bfloat16 [32768, 6], P(('expert', 'fsdp')), may hold values from 0.099609375 to 1
- w_gate: bfloat16 [8, 2048, 1408], P('expert', 'fsdp'), may hold values from -0.125 to 0.125
- w_up: bfloat16 [8, 2048, 1408], P('expert', 'fsdp'), may hold values from -0.125 to 0.125
- w_down: bfloat16 [8, 2048, 1408], P('expert', 'fsdp'), may hold values from -0.15625 to 0.15625
- cotangent: bfloat16 [32768, 2048], P(('expert', 'fsdp')), may hold values from -6 to 6
Outputs:
- output: bfloat16 [32768, 2048], P(('expert', 'fsdp'))
- grad_tokens: bfloat16 [32768, 2048], P(('expert', 'fsdp'))
- grad_gates: float32 [32768, 6], P(('expert', 'fsdp'))
- grad_w_gate: float32 [8, 2048, 1408], P('expert', 'fsdp')
- grad_w_up: float32 [8, 2048, 1408], P('expert', 'fsdp')
- grad_w_down: float32 [8, 2048, 1408], P('expert', 'fsdp')
Inputs may be any that keep to these rules, and one draw needn't show every extreme that they name: `expert_ids`: each row names 6 different experts. Among the tokens of one device at most 48 name any one expert whose number modulo 8 is below 1. On every device some such expert is named by exactly 48 of its tokens, and for every column one such expert is named by exactly 48 tokens of every device of that column.
All inputs are finite; a program needn't handle non-finite values.
Results may differ from a plain program's by a relative error of at most 0.013.
Values may be sent and summed in bfloat16 or wider, within the bound.
No kernel may reach another device: no remote copies, remote signals or barrier semaphores. Data moves between devices by JAX's collectives and lax.ppermute only.
A program may use at most 128 MiB of HBM per device.

v0:
```python
import jax
import jax.numpy as jnp
from jax import lax
from jax.sharding import PartitionSpec as P

EXPERTS = 64
TOP = 6
WAVE = 1
MOST = 48


def slot_tables(expert_ids, groups):
    per_index = EXPERTS // groups
    window = WAVE * groups
    tok_count = expert_ids.shape[0]
    flat_ids = expert_ids.reshape(-1)
    local_index = flat_ids % per_index
    is_live = local_index < WAVE
    window_slot = jnp.where(is_live, flat_ids // per_index * WAVE + local_index, window)
    onehot = (window_slot[:, None] == jnp.arange(window, dtype=jnp.int32)[None, :]).astype(
        jnp.int32
    )
    rank_in = jnp.sum((jnp.cumsum(onehot, axis=0) - 1) * onehot, axis=1)
    target = jnp.where(is_live, window_slot * MOST + rank_in, window * MOST)
    slot_ids = jnp.arange(tok_count * TOP, dtype=jnp.int32)
    source = (
        jnp.full((window * MOST,), tok_count * TOP, jnp.int32).at[target].set(slot_ids, mode="drop")
    )
    return (target, source)


def on_device(tokens, expert_ids, gate_vals, w_gate, w_up, w_down, cotangent):
    groups = lax.axis_size("expert")
    tok_count, model_width = tokens.shape
    target, source = slot_tables(expert_ids, groups)
    token_of = source // TOP
    zero_row = jnp.zeros((1, model_width), jnp.bfloat16)
    tokens_pad = jnp.concatenate([tokens, zero_row], axis=0)
    cot_pad = jnp.concatenate([cotangent, zero_row], axis=0)
    gate_pad = jnp.concatenate([gate_vals.reshape(-1), jnp.zeros((1,), jnp.bfloat16)], axis=0)
    send_rows = tokens_pad[token_of].reshape(groups, WAVE * MOST, model_width)
    arrived = lax.all_to_all(send_rows, "expert", split_axis=0, concat_axis=0, tiled=True)
    rows_in = arrived.reshape(groups, WAVE, MOST, model_width)
    full_gate, full_up, full_down = (
        lax.all_gather(w_gate, "fsdp", axis=1, tiled=True),
        lax.all_gather(w_up, "fsdp", axis=1, tiled=True),
        lax.all_gather(w_down, "fsdp", axis=1, tiled=True),
    )
    gate_pre = jnp.einsum("skmd,kdf->skmf", rows_in, full_gate, preferred_element_type=jnp.float32)
    up_pre = jnp.einsum("skmd,kdf->skmf", rows_in, full_up, preferred_element_type=jnp.float32)
    sigmoid_g = jax.nn.sigmoid(gate_pre)
    hidden = (gate_pre * sigmoid_g * up_pre).astype(jnp.bfloat16)
    expert_out = jnp.einsum(
        "skmf,kdf->skmd", hidden, full_down, preferred_element_type=jnp.float32
    ).astype(jnp.bfloat16)
    returned = lax.all_to_all(
        expert_out.reshape(groups, WAVE * MOST, model_width),
        "expert",
        split_axis=0,
        concat_axis=0,
        tiled=True,
    )
    back_pad = jnp.concatenate([returned.reshape(-1, model_width), zero_row], axis=0)
    slot_out = back_pad[target].reshape(tok_count, TOP, model_width).astype(jnp.float32)
    output = jnp.sum(gate_vals.astype(jnp.float32)[:, :, None] * slot_out, axis=1).astype(
        jnp.bfloat16
    )
    grad_gates = jnp.sum(cotangent.astype(jnp.float32)[:, None, :] * slot_out, axis=2)
    gate_rows = gate_pad[source].astype(jnp.float32)
    send_grad = (gate_rows[:, None] * cot_pad[token_of].astype(jnp.float32)).astype(jnp.bfloat16)
    grad_in = lax.all_to_all(
        send_grad.reshape(groups, WAVE * MOST, model_width),
        "expert",
        split_axis=0,
        concat_axis=0,
        tiled=True,
    )
    out_grad = grad_in.reshape(groups, WAVE, MOST, model_width)
    hidden_grad = jnp.einsum(
        "skmd,kdf->skmf", out_grad, full_down, preferred_element_type=jnp.float32
    )
    gate_grad = (hidden_grad * up_pre * sigmoid_g * (1.0 + gate_pre * (1.0 - sigmoid_g))).astype(
        jnp.bfloat16
    )
    up_grad = (hidden_grad * gate_pre * sigmoid_g).astype(jnp.bfloat16)
    row_grad = (
        jnp.einsum("skmf,kdf->skmd", gate_grad, full_gate, preferred_element_type=jnp.float32)
        + jnp.einsum("skmf,kdf->skmd", up_grad, full_up, preferred_element_type=jnp.float32)
    ).astype(jnp.bfloat16)
    grads_home = lax.all_to_all(
        row_grad.reshape(groups, WAVE * MOST, model_width),
        "expert",
        split_axis=0,
        concat_axis=0,
        tiled=True,
    )
    grads_pad = jnp.concatenate([grads_home.reshape(-1, model_width), zero_row], axis=0)
    grad_tokens = jnp.sum(
        grads_pad[target].reshape(tok_count, TOP, model_width).astype(jnp.float32), axis=1
    ).astype(jnp.bfloat16)
    term_gate = jnp.einsum("skmd,skmf->kdf", rows_in, gate_grad, preferred_element_type=jnp.float32)
    term_up = jnp.einsum("skmd,skmf->kdf", rows_in, up_grad, preferred_element_type=jnp.float32)
    term_down = jnp.einsum("skmd,skmf->kdf", out_grad, hidden, preferred_element_type=jnp.float32)
    grad_w_gate, grad_w_up, grad_w_down = (
        lax.psum_scatter(
            term_gate.astype(jnp.bfloat16), "fsdp", scatter_dimension=1, tiled=True
        ).astype(jnp.float32),
        lax.psum_scatter(
            term_up.astype(jnp.bfloat16), "fsdp", scatter_dimension=1, tiled=True
        ).astype(jnp.float32),
        lax.psum_scatter(
            term_down.astype(jnp.bfloat16), "fsdp", scatter_dimension=1, tiled=True
        ).astype(jnp.float32),
    )
    return (output, grad_tokens, grad_gates, grad_w_gate, grad_w_up, grad_w_down)


def solution(mesh):
    placed = (
        P(("expert", "fsdp"), None),
        P(("expert", "fsdp"), None),
        P(("expert", "fsdp"), None),
        P("expert", "fsdp", None),
        P("expert", "fsdp", None),
        P("expert", "fsdp", None),
        P(("expert", "fsdp"), None),
    )
    return jax.shard_map(
        on_device,
        mesh=mesh,
        in_specs=placed,
        out_specs=(
            P(("expert", "fsdp"), None),
            P(("expert", "fsdp"), None),
            P(("expert", "fsdp"), None),
            P("expert", "fsdp", None),
            P("expert", "fsdp", None),
            P("expert", "fsdp", None),
        ),
        check_vma=False,
    )
```

profile of v0, /device:TPU:0, one launch (start us, length us, event | category | flops | bytes accessed | tf_op | source)
XLA Modules:
  0.0 461.0 jit_solution(18036882781366785138)
XLA Ops:
  7.2 0.7 all-gather.8.cloned.1.call-update
  8.0 0.7 all-gather.6.cloned.1.call-update
  8.7 0.7 all-gather.4.cloned.1.call-update
  9.4 0.8 copy.20
  10.2 0.1 reshape.311
  10.4 0.1 reshape.313
  10.5 0.1 reshape.312
  10.7 0.8 copy.23
  11.5 0.2 reshape.321
  11.7 2.3 reduce-window.6
  14.0 0.3 slice_reduce_fusion
  14.3 0.2 reduce-window.9
  14.4 0.1 add_bitcast_fusion
  14.6 0.1 fusion.48
  14.7 6.2 %scatter_custom_fusion = s32[384]{0:T(512)S(1)} fusion(s32[1536]{0:T(1024)S(1)} %get-tuple-element.15, s32[1536]{0:T(1024)S(1)} %iota.11, s32[]{:T(128)} %constant.52.clone.1), kind=kCustom, calls=%fused_computation.94 | custom fusion | bytes 1540 | tf_op jit(solution)/shard_map/scatter | solution.py:27
  20.9 2.8 gather_fusion.2
  23.7 0.1 reshape.327
  23.8 0.1 concatenate.18
  23.9 2.5 gather_fusion.3
  26.4 1.5 fusion.15
  27.9 5.4 %all-to-all-start.2 = ((bf16[8,48,2048]{2,1,0:T(8,128)(2,1)}), bf16[8,48,2048]{2,1,0:T(8,128)(2,1)S(1)}, u32[]{:S(2)}, u32[]{:S(2)}) async-start(bf16[8,48,2048]{2,1,0:T(8,128)(2,1)} %fusion.15), calls=%async_computation.2 | async-start | bytes 3145728 | tf_op jit(solution)/shard_map/all_to_all | solution.py:71
  33.3 1.3 concatenate.15
  34.6 3.1 gather_fusion
  37.7 17.1 %all-to-all-done.2 = bf16[8,48,2048]{2,1,0:T(8,128)(2,1)S(1)} async-done(((bf16[8,48,2048]{2,1,0:T(8,128)(2,1)}), bf16[8,48,2048]{2,1,0:T(8,128)(2,1)S(1)}, u32[]{:S(2)}, u32[]{:S(2)}) %all-to-all-start.2) | async-done | bytes 1572896 | tf_op jit(solution)/shard_map/all_to_all | solution.py:71
  54.9 3.6 all-to-all-start
  58.5 0.0 reduce-scatter.8.cloned.1.call-start
  58.5 12.8 %all-gather.8.cloned.1.call-done = bf16[1,2048,1408]{2,1,0:T(8,128)(2,1)} async-done(((bf16[1,128,1408]{2,1,0:T(8,128)(2,1)}), bf16[1,2048,1408]{2,1,0:T(8,128)(2,1)}) %all-gather.8.cloned.1.call-update) | async-done | bytes 5767184 | tf_op jit(solution)/shard_map/all_gather | solution.py:47
  71.4 6.6 %fusion.22 = f32[8,1,48,1408]{3,2,0,1:T(8,128)} fusion(bf16[8,48,2048]{2,1,0:T(8,128)(2,1)S(1)} %all-to-all-done.2, bf16[1,2048,1408]{2,1,0:T(8,128)(2,1)} %all-gather.8.cloned.1.call-done), kind=kOutput, calls=%fused_computation.31 | convolution fusion | flops 2214592512 | bytes 9502720 | tf_op jit(solution)/shard_map/skmd,kdf->skmf/dot_general | solution.py:79
  78.0 2.0 all-to-all-done
  80.0 52.0 %all-gather.6.cloned.1.call-done = bf16[1,2048,1408]{2,1,0:T(8,128)(2,1)} async-done(((bf16[1,128,1408]{2,1,0:T(8,128)(2,1)}), bf16[1,2048,1408]{2,1,0:T(8,128)(2,1)}) %all-gather.6.cloned.1.call-update) | async-done | bytes 5767184 | tf_op jit(solution)/shard_map/all_gather | solution.py:46
  132.0 6.6 %fusion.19 = f32[8,1,48,1408]{3,2,0,1:T(8,128)} fusion(bf16[8,48,2048]{2,1,0:T(8,128)(2,1)S(1)} %all-to-all-done, bf16[1,2048,1408]{2,1,0:T(8,128)(2,1)} %all-gather.6.cloned.1.call-done), kind=kOutput, calls=%fused_computation.30 | convolution fusion | flops 2214592512 | bytes 9502720 | tf_op jit(solution)/shard_map/skmd,kdf->skmf/dot_general | solution.py:50
  138.6 54.0 %all-gather.4.cloned.1.call-done = bf16[1,2048,1408]{2,1,0:T(8,128)(2,1)} async-done(((bf16[1,128,1408]{2,1,0:T(8,128)(2,1)}), bf16[1,2048,1408]{2,1,0:T(8,128)(2,1)}) %all-gather.4.cloned.1.call-update) | async-done | bytes 5767184 | tf_op jit(solution)/shard_map/all_gather | solution.py:45
  192.6 7.9 %multiply_convert_fusion.1 = (bf16[8,1,48,1408]{3,2,0,1:T(8,128)(2,1)}, bf16[8,1,48,1408]{3,2,0,1:T(8,128)(2,1)S(1)}, bf16[8,1,48,1408]{3,2,0,1:T(8,128)(2,1)}) fusion(f32[8,1,48,1408]{3,2,0,1:T(8,128)} %fusion.22, f32[8,1,48,1408]{3,2,0,1:T(8,128)} %fusion.19, bf16[8,48,2048]{2,1,0:T(8,128)(2,1)S(1)} %all-to-all-done, ...), kind=kOutput, calls=%fused_computation.34 | convolution fusion | flops 2223243264 | bytes 14909440 | tf_op jit(solution)/shard_map/skmd,kdf->skmf/dot_general | solution.py:49
  200.5 1.0 copy-done.5
  201.5 5.2 %fusion.2 = bf16[1,2048,1408]{2,1,0:T(8,128)(2,1)} fusion(bf16[8,48,2048]{2,1,0:T(8,128)(2,1)S(1)} %all-to-all-done.2, bf16[8,1,48,1408]{3,2,0,1:T(8,128)(2,1)S(1)} %get-tuple-element.17), kind=kOutput, calls=%fused_computation.13 | convolution fusion | flops 2217476096 | bytes 8421376 | tf_op jit(solution)/shard_map/skmd,skmf->kdf/dot_general | solution.py:103
  206.7 0.2 reduce-scatter.4.cloned.1.call-start
  206.9 1.0 copy-done.7
  207.9 5.1 %fusion = bf16[1,2048,1408]{2,1,0:T(8,128)(2,1)} fusion(bf16[8,48,2048]{2,1,0:T(8,128)(2,1)S(1)} %all-to-all-done, bf16[8,1,48,1408]{3,2,0,1:T(8,128)(2,1)S(1)} %copy-done.7), kind=kOutput, calls=%fused_computation.11 | convolution fusion | flops 2217476096 | bytes 8421376 | tf_op jit(solution)/shard_map/skmd,skmf->kdf/dot_general | solution.py:101
  213.1 1.2 copy-done.4
  214.3 5.1 %fusion.1 = bf16[1,2048,1408]{2,1,0:T(8,128)(2,1)} fusion(bf16[8,48,2048]{2,1,0:T(8,128)(2,1)S(1)} %all-to-all-done, bf16[8,1,48,1408]{3,2,0,1:T(8,128)(2,1)S(1)} %copy-done.4), kind=kOutput, calls=%fused_computation.12 | convolution fusion | flops 2217476096 | bytes 8421376 | tf_op jit(solution)/shard_map/skmd,skmf->kdf/dot_general | solution.py:102
  219.4 1.2 copy-done.6
  220.6 7.8 %fusion.27 = bf16[8,48,2048]{2,1,0:T(8,128)(2,1)} fusion(bf16[1,2048,1408]{2,1,0:T(8,128)(2,1)} %all-gather.8.cloned.1.call-done, bf16[8,1,48,1408]{3,2,0,1:T(8,128)(2,1)S(1)} %copy-done.6), kind=kOutput, calls=%fused_computation.32 | convolution fusion | flops 2215378944 | bytes 8421376 | tf_op jit(solution)/shard_map/skmf,kdf->skmd/dot_general | solution.py:53
  228.4 4.6 all-to-all-start.1
  232.9 5.2 %fusion.7 = f32[8,48,2048]{2,1,0:T(8,128)S(1)} fusion(bf16[1,2048,1408]{2,1,0:T(8,128)(2,1)} %all-gather.6.cloned.1.call-done, bf16[8,1,48,1408]{3,2,0,1:T(8,128)(2,1)} %get-tuple-element.18), kind=kOutput, calls=%fused_computation.18 | convolution fusion | flops 2214592512 | bytes 9994240 | tf_op jit(solution)/shard_map/skmf,kdf->skmd/dot_general | solution.py:88
  238.2 3.8 add_convert_fusion
  242.0 12.5 %all-to-all-done.1 = bf16[8,48,2048]{2,1,0:T(8,128)(2,1)S(1)} async-done(((bf16[8,48,2048]{2,1,0:T(8,128)(2,1)}), bf16[8,48,2048]{2,1,0:T(8,128)(2,1)S(1)}, u32[]{:S(2)}, u32[]{:S(2)}) %all-to-all-start.1) | async-done | bytes 1572896 | tf_op jit(solution)/shard_map/all_to_all | solution.py:56
  254.5 4.3 all-to-all-start.3
  258.8 0.1 copy.19
  259.0 1.6 convert_element_type.110
  260.6 0.2 concatenate.16
  260.8 19.6 %all-to-all-done.3 = bf16[8,48,2048]{2,1,0:T(8,128)(2,1)} async-done(((bf16[8,48,2048]{2,1,0:T(8,128)(2,1)}), bf16[8,48,2048]{2,1,0:T(8,128)(2,1)}, u32[]{:S(2)}, u32[]{:S(2)}) %all-to-all-start.3) | async-done | bytes 1572896 | tf_op jit(solution)/shard_map/all_to_all | solution.py:90
  280.4 1.5 concatenate.19
  281.9 7.1 %gather_fusion.4 = bf16[1536,2048]{1,0:T(8,128)(2,1)} fusion(bf16[385,2048]{1,0:T(8,128)(2,1)S(1)} %concatenate.19, s32[2048]{0:T(1024)S(1)} %pad_clamp_fusion), kind=kCustom, calls=%fused_computation.4 | custom fusion | bytes 12589056 | tf_op jit(solution)/shard_map/gather | solution.py:99
  289.0 11.0 %reshape.325 = bf16[256,6,2048]{2,1,0:T(8,128)(2,1)} reshape(bf16[1536,2048]{1,0:T(8,128)(2,1)} %gather_fusion.4) | data formatting | bytes 12582912 | tf_op jit(solution)/shard_map/reshape | solution.py:99
  300.0 9.7 %reduce_sum.44 = bf16[256,2048]{1,0:T(8,128)(2,1)} reduce(bf16[256,6,2048]{2,1,0:T(8,128)(2,1)} %reshape.325, bf16[]{:T(256)} %constant.31.clone.1), dimensions={1}, to_apply=%region_5.6 | reduce | flops 2621440 | bytes 7340034 | tf_op jit(solution)/shard_map/reduce_sum | solution.py:98
  309.8 7.1 %gather_fusion.1 = bf16[1536,2048]{1,0:T(8,128)(2,1)} fusion(bf16[385,2048]{1,0:T(8,128)(2,1)S(1)} %concatenate.16, s32[2048]{0:T(1024)S(1)} %pad_clamp_fusion), kind=kCustom, calls=%fused_computation.1 | custom fusion | bytes 12589056 | tf_op jit(solution)/shard_map/gather | solution.py:64
  316.9 12.0 %reshape.326 = f32[256,6,2048]{2,1,0:T(8,128)} reshape(bf16[1536,2048]{1,0:T(8,128)(2,1)} %gather_fusion.1) | data formatting | bytes 18874368 | tf_op jit(solution)/shard_map/convert_element_type | solution.py:64
  328.9 11.9 %multiply_reduce_fusion = (f32[256,6]{1,0:T(8,128)S(1)}, bf16[256,2048]{1,0:T(8,128)(2,1)}) fusion(f32[256,6,2048]{2,1,0:T(8,128)} %reshape.326, f32[256,2048]{1,0:T(8,128)S(1)} %copy-done, f32[256,6]{1,0:T(8,128)S(1)} %copy.19), kind=kLoop, calls=%fused_computation.6 | loop fusion | flops 12057088 | bytes 15740928 | tf_op jit(solution)/shard_map/reduce_sum | solution.py:68
  340.8 0.7 copy.24
  341.5 1.9 convert_element_type.119
  343.4 26.1 %reduce-scatter.4.cloned.1.call-done = bf16[1,128,1408]{2,1,0:T(8,128)(2,1)} async-done(((bf16[1,2048,1408]{2,1,0:T(8,128)(2,1)}), bf16[1,128,1408]{2,1,0:T(8,128)(2,1)}) %reduce-scatter.4.cloned.1.call-update) | async-done | bytes 360464 | tf_op jit(solution)/shard_map/reduce_scatter | solution.py:105
  369.5 1.9 convert_element_type.113
  371.4 80.9 %reduce-scatter.6.cloned.1.call-done = bf16[1,128,1408]{2,1,0:T(8,128)(2,1)} async-done(((bf16[1,2048,1408]{2,1,0:T(8,128)(2,1)}), bf16[1,128,1408]{2,1,0:T(8,128)(2,1)}) %reduce-scatter.6.cloned.1.call-update) | async-done | bytes 360464 | tf_op jit(solution)/shard_map/reduce_scatter | solution.py:108
  452.3 1.9 convert_element_type.116
  (36 shorter events, 0.3 us)
Async XLA Ops:
  7.2 16.6 %copy-start.1 = (bf16[256,2048]{1,0:T(8,128)(2,1)S(1)}, bf16[256,2048]{1,0:T(8,128)(2,1)}, u32[]{:S(2)}) copy-start(bf16[256,2048]{1,0:T(8,128)(2,1)} %param.13) | copy-start | bytes 3145732
  7.2 64.2 %all-gather.8.cloned.1.call-start = ((), (), s32[]{:S(2)}) async-start(), calls=%async_computation.9 | async-start | bytes 6127616 | tf_op jit(solution)/shard_map/all_gather | solution.py:47
  7.9 124.1 %all-gather.6.cloned.1.call-start = ((), (), s32[]{:S(2)}) async-start(), calls=%async_computation.8 | async-start | bytes 6127616 | tf_op jit(solution)/shard_map/all_gather | solution.py:46
  8.7 184.0 %all-gather.4.cloned.1.call-start = ((), (), s32[]{:S(2)}) async-start(), calls=%async_computation.7 | async-start | bytes 6127616 | tf_op jit(solution)/shard_map/all_gather | solution.py:45
  27.9 27.0 %all-to-all-start.2 = ((bf16[8,48,2048]{2,1,0:T(8,128)(2,1)}), bf16[8,48,2048]{2,1,0:T(8,128)(2,1)S(1)}, u32[]{:S(2)}, u32[]{:S(2)}) async-start(bf16[8,48,2048]{2,1,0:T(8,128)(2,1)} %fusion.15), calls=%async_computation.2 | async-start | bytes 3145728 | tf_op jit(solution)/shard_map/all_to_all | solution.py:71
  54.9 25.1 %all-to-all-start = ((bf16[8,48,2048]{2,1,0:T(8,128)(2,1)}), bf16[8,48,2048]{2,1,0:T(8,128)(2,1)S(1)}, u32[]{:S(2)}, u32[]{:S(2)}) async-start(bf16[8,48,2048]{2,1,0:T(8,128)(2,1)} %bitcast.1), calls=%async_computation | async-start | bytes 3145728 | tf_op jit(solution)/shard_map/all_to_all | solution.py:42
  58.5 283.0 %reduce-scatter.8.cloned.1.call-start = ((), (), s32[]{:S(2)}) async-start(), calls=%async_computation.12 | async-start | bytes 6127616 | tf_op jit(solution)/shard_map/reduce_scatter | solution.py:111
  200.5 1.0 copy-start.5
  206.7 1.2 copy-start.7
  206.7 162.8 %reduce-scatter.4.cloned.1.call-start = ((), (), s32[]{:S(2)}) async-start(), calls=%async_computation.10 | async-start | bytes 6127616 | tf_op jit(solution)/shard_map/reduce_scatter | solution.py:105
  213.0 1.2 copy-start.4
  213.1 239.2 %reduce-scatter.6.cloned.1.call-start = ((), (), s32[]{:S(2)}) async-start(), calls=%async_computation.11 | async-start | bytes 6127616 | tf_op jit(solution)/shard_map/reduce_scatter | solution.py:108
  219.4 1.2 copy-start.6
  228.4 9.8 %slice-start = ((s8[5767168]{0:T(1024)(128)(4,1)}), s8[1572864]{0:T(1024)(128)(4,1)S(1)}, s32[]{:S(2)}) async-start(s8[5767168]{0:T(1024)(128)(4,1)} %bitcast.111), calls=%async_computation.13 | async-start | bytes 3145728
  228.4 26.1 %all-to-all-start.1 = ((bf16[8,48,2048]{2,1,0:T(8,128)(2,1)}), bf16[8,48,2048]{2,1,0:T(8,128)(2,1)S(1)}, u32[]{:S(2)}, u32[]{:S(2)}) async-start(bf16[8,48,2048]{2,1,0:T(8,128)(2,1)} %fusion.27), calls=%async_computation.1 | async-start | bytes 3145728 | tf_op jit(solution)/shard_map/all_to_all | solution.py:56
  232.9 5.2 %slice-start.1 = ((s8[5767168]{0:T(1024)(128)(4,1)}), s8[4194304]{0:T(1024)(128)(4,1)S(1)}, s32[]{:S(2)}) async-start(s8[5767168]{0:T(1024)(128)(4,1)} %bitcast.111), calls=%async_computation.14 | async-start | bytes 8388608
  232.9 5.2 %copy-start.8 = (bf16[8,1,48,1408]{3,2,0,1:T(8,128)(2,1)S(1)}, bf16[8,1,48,1408]{3,2,0,1:T(8,128)(2,1)}, u32[]{:S(2)}) copy-start(bf16[8,1,48,1408]{3,2,0,1:T(8,128)(2,1)} %get-tuple-element.16) | copy-start | bytes 3244036
  242.0 16.8 %copy-start.3 = (bf16[256,6]{0,1:T(8,128)(2,1)S(1)}, bf16[256,6]{0,1:T(8,128)(2,1)}, u32[]{:S(2)}) copy-start(bf16[256,6]{0,1:T(8,128)(2,1)} %param.9) | copy-start | bytes 9220
  242.0 16.9 %copy-start.2 = (bf16[256,2048]{1,0:T(8,128)(2,1)S(1)}, bf16[256,2048]{1,0:T(8,128)(2,1)}, u32[]{:S(2)}) copy-start(bf16[256,2048]{1,0:T(8,128)(2,1)} %param.13) | copy-start | bytes 3145732
  254.5 25.9 %all-to-all-start.3 = ((bf16[8,48,2048]{2,1,0:T(8,128)(2,1)}), bf16[8,48,2048]{2,1,0:T(8,128)(2,1)}, u32[]{:S(2)}, u32[]{:S(2)}) async-start(bf16[8,48,2048]{2,1,0:T(8,128)(2,1)} %add_convert_fusion), calls=%async_computation.3 | async-start | bytes 3145728 | tf_op jit(solution)/shard_map/all_to_all | solution.py:90
  316.9 12.0 %copy-start = (f32[256,2048]{1,0:T(8,128)S(1)}, f32[256,2048]{1,0:T(8,128)}, u32[]{:S(2)}) copy-start(f32[256,2048]{1,0:T(8,128)} %convert_element_type.110) | copy-start | bytes 6291460
Sparse Core Ops, SparseCore 0:
  10.1 61.1 all-gather.7
  73.5 58.4 all-gather.5
  134.1 58.4 all-gather.3
  206.8 79.7 reduce-scatter.7
  289.8 79.5 reduce-scatter.3
  372.7 79.5 reduce-scatter.5
where the time goes:
time: 463 us; the launch traced here: 461 us
  waiting for transfers between devices  279 us (60%)
  local copies, waits for them, and re-layouts  62.6 us (14%)
  matrix products  53.3 us (12%)
  other arithmetic  33.2 us (7%)
  starting transfers between devices  18.3 us (4%)
  between operations  14.4 us (3%)
    reduce_scatter x1, waiting for transfers between devices, on_device(): lax.psum_scatter(term_up.astype(jnp.bfloat16), 'fsdp', scatter_dimension=...  80.9 us
    all_gather x1, waiting for transfers between devices, on_device(): lax.all_gather(w_gate, 'fsdp', axis=1, tiled=True)  54 us
    all_gather x1, waiting for transfers between devices, on_device(): lax.all_gather(w_up, 'fsdp', axis=1, tiled=True)  52 us
    reduce_scatter x1, waiting for transfers between devices, on_device(): lax.psum_scatter(term_gate.astype(jnp.bfloat16), 'fsdp', scatter_dimensio...  26.1 us
    all_to_all x1, waiting for transfers between devices, on_device(): lax.all_to_all(row_grad.reshape(groups, WAVE * MOST, model_width), 'exper...  19.6 us
    all_to_all x1, waiting for transfers between devices, on_device(): lax.all_to_all(send_grad.reshape(groups, WAVE * MOST, model_width), 'expe...  17.1 us
    all_gather x1, waiting for transfers between devices, on_device(): lax.all_gather(w_down, 'fsdp', axis=1, tiled=True)  12.8 us
    all_to_all x1, waiting for transfers between devices, on_device(): lax.all_to_all(expert_out.reshape(groups, WAVE * MOST, model_width), 'exp...  12.5 us
  transfers between devices with their start and end apart: 10, of which 9 were waited for; matrix products, arithmetic and copies ran while one was open for 28% of the time, Pallas kernels for 0%

commit v1 on v0

--- a/solution.py
+++ b/solution.py
@@ -7,6 +7,13 @@
 TOP = 6
 WAVE = 1
 MOST = 48
+
+
+def runs_deliver(w_in):
+    high = lax.axis_size("fsdp")
+    response = jnp.stack(high * [w_in])
+    current_block = lax.all_to_all(response, "fsdp", 0, 0)
+    return jnp.concatenate(current_block, 1)
 
 
 def slot_tables(expert_ids, groups):
@@ -44,7 +51,7 @@
     full_gate, full_up, full_down = (
         lax.all_gather(w_gate, "fsdp", axis=1, tiled=True),
         lax.all_gather(w_up, "fsdp", axis=1, tiled=True),
-        lax.all_gather(w_down, "fsdp", axis=1, tiled=True),
+        runs_deliver(w_down),
     )
     gate_pre = jnp.einsum("skmd,kdf->skmf", rows_in, full_gate, preferred_element_type=jnp.float32)
     up_pre = jnp.einsum("skmd,kdf->skmf", rows_in, full_up, preferred_element_type=jnp.float32)

time: 463 us -> 460 us (level)
  waiting for transfers between devices: 279 us -> 246 us
  blocking collectives: 0 us -> 27.1 us
    all_to_all x1, waiting for transfers between devices: 17.1 us -> 90 us  [runs_deliver(): current_block = lax.all_to_all(response, 'fsdp', 0, 0)]
    all_gather x1, waiting for transfers between devices: 54 us -> 0.34 us  [on_device(): lax.all_gather(w_gate, 'fsdp', axis=1, tiled=True)]
    all_gather x1, waiting for transfers between devices: 52 us -> 0.01 us  [on_device(): lax.all_gather(w_up, 'fsdp', axis=1, tiled=True)]
    all_to_all x0 -> x1, blocking collectives: none -> 27.1 us  [on_device(): lax.all_to_all(send_grad.reshape(groups, WAVE * MOST, model_width), 'expe...]
    reduce_scatter x1, waiting for transfers between devices: 26.1 us -> 45 us  [on_device(): lax.psum_scatter(term_gate.astype(jnp.bfloat16), 'fsdp', scatter_dimensio...]
    all_gather x1 -> x0, waiting for transfers between devices: 12.8 us -> none  [on_device(): lax.all_gather(w_down, 'fsdp', axis=1, tiled=True)]
    all_to_all x1, waiting for transfers between devices: 12.5 us -> 0.01 us  [on_device(): lax.all_to_all(expert_out.reshape(groups, WAVE * MOST, model_width), 'exp...]
    all_to_all x1, waiting for transfers between devices: 1.99 us -> 14.3 us  [on_device(): lax.all_to_all(send_rows, 'expert', split_axis=0, concat_axis=0, tiled=True)]
  transfers between devices with their start and end apart: 10 -> 9, of which waited for: 9 -> 6; matrix products, arithmetic and copies ran while one was open for 28% -> 29% of each run, Pallas kernels for 0% -> 0%
where the time goes in v1:
time: 460 us; the launch traced here: 459 us
  waiting for transfers between devices  246 us (53%)
  local copies, waits for them, and re-layouts  64.7 us (14%)
  matrix products  53.5 us (12%)
  other arithmetic  33.3 us (7%)
  blocking collectives  27.1 us (6%)
  starting transfers between devices  20.6 us (4%)
  between operations  14.1 us (3%)
    all_to_all x1, waiting for transfers between devices, runs_deliver(): current_block = lax.all_to_all(response, 'fsdp', 0, 0)  90 us
    reduce_scatter x1, waiting for transfers between devices, on_device(): lax.psum_scatter(term_up.astype(jnp.bfloat16), 'fsdp', scatter_dimension=...  80.7 us
    reduce_scatter x1, waiting for transfers between devices, on_device(): lax.psum_scatter(term_gate.astype(jnp.bfloat16), 'fsdp', scatter_dimensio...  45 us
    all_to_all x1, blocking collectives, on_device(): lax.all_to_all(send_grad.reshape(groups, WAVE * MOST, model_width), 'expe...  27.1 us
    all_to_all x1, waiting for transfers between devices, on_device(): lax.all_to_all(send_rows, 'expert', split_axis=0, concat_axis=0, tiled=True)  14.3 us
    all_to_all x1, waiting for transfers between devices, on_device(): lax.all_to_all(row_grad.reshape(groups, WAVE * MOST, model_width), 'exper...  13.8 us
    convert_element_type x1, local copies, waits for them, and re-layouts, on_device(): back_pad[target].reshape(tok_count, TOP, model_width).astype(jnp.float32)  12 us
    reduce_sum x1, other arithmetic, on_device(): jnp.sum(cotangent.astype(jnp.float32)[:, None, :] * slot_out, axis=2)  11.9 us
  transfers between devices with their start and end apart: 9, of which 6 were waited for; matrix products, arithmetic and copies ran while one was open for 29% of the time, Pallas kernels for 0%

profile of v1, /device:TPU:0, one launch (start us, length us, event | category | flops | bytes accessed | tf_op | source)
XLA Modules:
  0.0 458.8 jit_solution(13977984579217965506)
XLA Ops:
  7.2 0.0 all-gather.5.cloned.1.call-start
  7.2 0.7 all-gather.5.cloned.1.call-update
  7.9 0.0 all-gather.3.cloned.1.call-start
  8.0 0.7 all-gather.3.cloned.1.call-update
  8.7 0.8 copy.20
  9.5 0.1 reshape.319
  9.6 0.1 reshape.318
  9.8 0.1 reshape.317
  10.0 2.3 reduce-window.6
  12.2 0.3 slice_reduce_fusion
  12.5 0.2 reduce-window.9
  12.7 0.8 copy.23
  13.5 0.2 reshape.327
  13.7 0.1 add_bitcast_fusion
  13.8 0.1 fusion.38
  13.9 6.2 %scatter_custom_fusion = s32[384]{0:T(512)S(1)} fusion(s32[1536]{0:T(1024)S(1)} %get-tuple-element.15, s32[1536]{0:T(1024)S(1)} %iota.11, s32[]{:T(128)} %constant.52.clone.1), kind=kCustom, calls=%fused_computation.90 | custom fusion | bytes 1540 | tf_op jit(solution)/shard_map/scatter | solution.py:34
  20.2 2.8 gather_fusion.2
  23.0 0.1 reshape.333
  23.1 0.1 concatenate.18
  23.2 2.5 gather_fusion.3
  25.6 0.3 fusion.11
  26.0 27.1 %all_to_all.25 = bf16[8,48,2048]{2,1,0:T(8,128)(2,1)S(1)} all-to-all(bf16[8,48,2048]{2,1,0:T(8,128)(2,1)S(1)} %fusion.11), channel_id=1, replica_groups=mesh['expert'=8,'fsdp'=16] {'expert'}, dimensions={0} | all-to-all | bytes 3145728 | tf_op jit(solution)/shard_map/all_to_all | solution.py:78
  53.1 3.1 stack.2
  56.2 7.1 %all-to-all-start.1 = ((bf16[16,1,128,1408]{3,2,1,0:T(8,128)(2,1)}), bf16[16,1,128,1408]{3,2,1,0:T(8,128)(2,1)}, u32[]{:S(2)}, u32[]{:S(2)}) async-start(bf16[16,1,128,1408]{3,2,1,0:T(8,128)(2,1)} %stack.2), calls=%async_computation.1 | async-start | bytes 11534336 | tf_op jit(solution)/shard_map/all_to_all | solution.py:15
  63.3 1.3 concatenate.15
  64.6 3.1 gather_fusion
  67.7 90.0 %all-to-all-done.1 = bf16[16,1,128,1408]{3,2,1,0:T(8,128)(2,1)} async-done(((bf16[16,1,128,1408]{3,2,1,0:T(8,128)(2,1)}), bf16[16,1,128,1408]{3,2,1,0:T(8,128)(2,1)}, u32[]{:S(2)}, u32[]{:S(2)}) %all-to-all-start.1) | async-done | bytes 5767200 | tf_op jit(solution)/shard_map/all_to_all | solution.py:15
  157.8 5.0 %all-to-all-start = ((bf16[8,48,2048]{2,1,0:T(8,128)(2,1)}), bf16[8,48,2048]{2,1,0:T(8,128)(2,1)S(1)}, u32[]{:S(2)}, u32[]{:S(2)}) async-start(bf16[8,48,2048]{2,1,0:T(8,128)(2,1)} %bitcast.1), calls=%async_computation | async-start | bytes 3145728 | tf_op jit(solution)/shard_map/all_to_all | solution.py:49
  162.8 0.2 reduce-scatter.8.cloned.1.call-start
  163.0 7.1 %convolution_bitcast_fusion = f32[8,1,48,1408]{3,2,0,1:T(8,128)} fusion(bf16[8,48,2048]{2,1,0:T(8,128)(2,1)S(1)} %all_to_all.25, bf16[2048,1408,1]{1,0,2:T(8,128)(2,1)} %bitcast.17), kind=kOutput, calls=%fused_computation.27 | convolution fusion | flops 2214592512 | bytes 9502720 | tf_op jit(solution)/shard_map/skmd,kdf->skmf/dot_general | solution.py:86
  170.1 14.3 %all-to-all-done = bf16[8,48,2048]{2,1,0:T(8,128)(2,1)S(1)} async-done(((bf16[8,48,2048]{2,1,0:T(8,128)(2,1)}), bf16[8,48,2048]{2,1,0:T(8,128)(2,1)S(1)}, u32[]{:S(2)}, u32[]{:S(2)}) %all-to-all-start) | async-done | bytes 1572896 | tf_op jit(solution)/shard_map/all_to_all | solution.py:49
  184.3 6.6 %fusion.15 = f32[8,1,48,1408]{3,2,0,1:T(8,128)} fusion(bf16[8,48,2048]{2,1,0:T(8,128)(2,1)S(1)} %all-to-all-done, bf16[1,2048,1408]{2,1,0:T(8,128)(2,1)} %all-gather.5.cloned.1.call-done), kind=kOutput, calls=%fused_computation.26 | convolution fusion | flops 2214592512 | bytes 9502720 | tf_op jit(solution)/shard_map/skmd,kdf->skmf/dot_general | solution.py:57
  191.0 0.3 all-gather.3.cloned.1.call-done
  191.3 8.0 %multiply_convert_fusion.1 = (bf16[8,1,48,1408]{3,2,0,1:T(8,128)(2,1)}, bf16[8,1,48,1408]{3,2,0,1:T(8,128)(2,1)S(1)}, bf16[8,1,48,1408]{3,2,0,1:T(8,128)(2,1)}) fusion(f32[8,1,48,1408]{3,2,0,1:T(8,128)} %convolution_bitcast_fusion, f32[8,1,48,1408]{3,2,0,1:T(8,128)} %fusion.15, bf16[8,48,2048]{2,1,0:T(8,128)(2,1)S(1)} %all-to-all-done, ...), kind=kOutput, calls=%fused_computation.30 | convolution fusion | flops 2223243264 | bytes 14909440 | tf_op jit(solution)/shard_map/skmd,kdf->skmf/dot_general | solution.py:56
  199.2 1.0 copy-done.6
  200.3 5.1 %fusion.2 = bf16[1,2048,1408]{2,1,0:T(8,128)(2,1)} fusion(bf16[8,48,2048]{2,1,0:T(8,128)(2,1)S(1)} %all_to_all.25, bf16[8,1,48,1408]{3,2,0,1:T(8,128)(2,1)S(1)} %get-tuple-element.17), kind=kOutput, calls=%fused_computation.13 | convolution fusion | flops 2217476096 | bytes 8421376 | tf_op jit(solution)/shard_map/skmd,skmf->kdf/dot_general | solution.py:110
  205.4 0.0 reduce-scatter.4.cloned.1.call-start
  205.5 1.2 copy-done.8
  206.7 5.1 %fusion = bf16[1,2048,1408]{2,1,0:T(8,128)(2,1)} fusion(bf16[8,48,2048]{2,1,0:T(8,128)(2,1)S(1)} %all-to-all-done, bf16[8,1,48,1408]{3,2,0,1:T(8,128)(2,1)S(1)} %copy-done.8), kind=kOutput, calls=%fused_computation.11 | convolution fusion | flops 2217476096 | bytes 8421376 | tf_op jit(solution)/shard_map/skmd,skmf->kdf/dot_general | solution.py:108
  211.8 0.0 reduce-scatter.6.cloned.1.call-start
  211.9 1.2 copy-done.5
  213.0 5.1 %fusion.1 = bf16[1,2048,1408]{2,1,0:T(8,128)(2,1)} fusion(bf16[8,48,2048]{2,1,0:T(8,128)(2,1)S(1)} %all-to-all-done, bf16[8,1,48,1408]{3,2,0,1:T(8,128)(2,1)S(1)} %copy-done.5), kind=kOutput, calls=%fused_computation.12 | convolution fusion | flops 2217476096 | bytes 8421376 | tf_op jit(solution)/shard_map/skmd,skmf->kdf/dot_general | solution.py:109
  218.2 4.8 %fusion.3 = f32[8,48,2048]{2,1,0:T(8,128)S(1)} fusion(bf16[1,2048,1408]{2,1,0:T(8,128)(2,1)} %all-gather.5.cloned.1.call-done, bf16[8,1,48,1408]{3,2,0,1:T(8,128)(2,1)S(1)} %copy-done.5), kind=kOutput, calls=%fused_computation.14 | convolution fusion | flops 2214592512 | bytes 9994240 | tf_op jit(solution)/shard_map/skmf,kdf->skmd/dot_general | solution.py:95
  223.1 3.8 add_convert_fusion
  226.9 4.5 all-to-all-start.4
  231.5 7.7 %convolution_convert_fusion = bf16[8,48,2048]{2,1,0:T(8,128)(2,1)} fusion(bf16[2048,1408,1]{1,0,2:T(8,128)(2,1)} %bitcast.17, bf16[8,1,48,1408]{3,2,0,1:T(8,128)(2,1)S(1)} %copy-done.7), kind=kOutput, calls=%fused_computation.28 | convolution fusion | flops 2215378944 | bytes 8421376 | tf_op jit(solution)/shard_map/skmf,kdf->skmd/dot_general | solution.py:60
  239.2 13.8 %all-to-all-done.4 = bf16[8,48,2048]{2,1,0:T(8,128)(2,1)S(1)} async-done(((bf16[8,48,2048]{2,1,0:T(8,128)(2,1)}), bf16[8,48,2048]{2,1,0:T(8,128)(2,1)S(1)}, u32[]{:S(2)}, u32[]{:S(2)}) %all-to-all-start.4) | async-done | bytes 1572896 | tf_op jit(solution)/shard_map/all_to_all | solution.py:97
  253.0 3.6 all-to-all-start.2
  256.6 2.9 convert_element_type.110
  259.5 0.1 copy.19
  259.7 1.5 concatenate.19
  261.2 7.0 %gather_fusion.4 = bf16[1536,2048]{1,0:T(8,128)(2,1)} fusion(bf16[385,2048]{1,0:T(8,128)(2,1)S(1)} %concatenate.19, s32[2048]{0:T(1024)S(1)} %pad_clamp_fusion), kind=kCustom, calls=%fused_computation.4 | custom fusion | bytes 12589056 | tf_op jit(solution)/shard_map/gather | solution.py:106
  268.3 11.0 %reshape.331 = bf16[256,6,2048]{2,1,0:T(8,128)(2,1)} reshape(bf16[1536,2048]{1,0:T(8,128)(2,1)} %gather_fusion.4) | data formatting | bytes 12582912 | tf_op jit(solution)/shard_map/reshape | solution.py:106
  279.2 9.8 %reduce_sum.44 = bf16[256,2048]{1,0:T(8,128)(2,1)} reduce(bf16[256,6,2048]{2,1,0:T(8,128)(2,1)} %reshape.331, bf16[]{:T(256)} %constant.31.clone.1), dimensions={1}, to_apply=%region_5.6 | reduce | flops 2621440 | bytes 7340034 | tf_op jit(solution)/shard_map/reduce_sum | solution.py:105
  289.1 0.2 concatenate.16
  289.3 7.1 %gather_fusion.1 = bf16[1536,2048]{1,0:T(8,128)(2,1)} fusion(bf16[385,2048]{1,0:T(8,128)(2,1)S(1)} %concatenate.16, s32[2048]{0:T(1024)S(1)} %pad_clamp_fusion), kind=kCustom, calls=%fused_computation.1 | custom fusion | bytes 12589056 | tf_op jit(solution)/shard_map/gather | solution.py:71
  296.3 12.0 %reshape.332 = f32[256,6,2048]{2,1,0:T(8,128)} reshape(bf16[1536,2048]{1,0:T(8,128)(2,1)} %gather_fusion.1) | data formatting | bytes 18874368 | tf_op jit(solution)/shard_map/convert_element_type | solution.py:71
  308.4 11.9 %multiply_reduce_fusion = (f32[256,6]{1,0:T(8,128)S(1)}, bf16[256,2048]{1,0:T(8,128)(2,1)}) fusion(f32[256,6,2048]{2,1,0:T(8,128)} %reshape.332, f32[256,2048]{1,0:T(8,128)S(1)} %copy-done, f32[256,6]{1,0:T(8,128)S(1)} %copy.19), kind=kLoop, calls=%fused_computation.6 | loop fusion | flops 12057088 | bytes 15740928 | tf_op jit(solution)/shard_map/reduce_sum | solution.py:75
  320.2 0.7 copy.24
  320.9 1.9 convert_element_type.119
  322.8 45.0 %reduce-scatter.4.cloned.1.call-done = bf16[1,128,1408]{2,1,0:T(8,128)(2,1)} async-done(((bf16[1,2048,1408]{2,1,0:T(8,128)(2,1)}), bf16[1,128,1408]{2,1,0:T(8,128)(2,1)}) %reduce-scatter.4.cloned.1.call-update) | async-done | bytes 360464 | tf_op jit(solution)/shard_map/reduce_scatter | solution.py:112
  367.8 1.9 convert_element_type.113
  369.7 80.7 %reduce-scatter.6.cloned.1.call-done = bf16[1,128,1408]{2,1,0:T(8,128)(2,1)} async-done(((bf16[1,2048,1408]{2,1,0:T(8,128)(2,1)}), bf16[1,128,1408]{2,1,0:T(8,128)(2,1)}) %reduce-scatter.6.cloned.1.call-update) | async-done | bytes 360464 | tf_op jit(solution)/shard_map/reduce_scatter | solution.py:115
  450.4 1.9 convert_element_type.116
  (37 shorter events, 0.2 us)
Async XLA Ops:
  7.2 15.9 %copy-start.2 = (bf16[256,2048]{1,0:T(8,128)(2,1)S(1)}, bf16[256,2048]{1,0:T(8,128)(2,1)}, u32[]{:S(2)}) copy-start(bf16[256,2048]{1,0:T(8,128)(2,1)} %param.13) | copy-start | bytes 3145732
  7.2 177.2 %all-gather.5.cloned.1.call-start = ((), (), s32[]{:S(2)}) async-start(), calls=%async_computation.9 | async-start | bytes 6127616 | tf_op jit(solution)/shard_map/all_gather | solution.py:53
  7.9 183.4 %all-gather.3.cloned.1.call-start = ((), (), s32[]{:S(2)}) async-start(), calls=%async_computation.8 | async-start | bytes 6127616 | tf_op jit(solution)/shard_map/all_gather | solution.py:52
  26.0 27.1 %copy-start.3 = (bf16[1,128,1408]{2,1,0:T(8,128)(2,1)S(1)}, bf16[1,128,1408]{2,1,0:T(8,128)(2,1)}, u32[]{:S(2)}) copy-start(bf16[1,128,1408]{2,1,0:T(8,128)(2,1)} %param.12) | copy-start | bytes 1081348
  56.2 101.5 %all-to-all-start.1 = ((bf16[16,1,128,1408]{3,2,1,0:T(8,128)(2,1)}), bf16[16,1,128,1408]{3,2,1,0:T(8,128)(2,1)}, u32[]{:S(2)}, u32[]{:S(2)}) async-start(bf16[16,1,128,1408]{3,2,1,0:T(8,128)(2,1)} %stack.2), calls=%async_computation.1 | async-start | bytes 11534336 | tf_op jit(solution)/shard_map/all_to_all | solution.py:15
  157.8 26.6 %all-to-all-start = ((bf16[8,48,2048]{2,1,0:T(8,128)(2,1)}), bf16[8,48,2048]{2,1,0:T(8,128)(2,1)S(1)}, u32[]{:S(2)}, u32[]{:S(2)}) async-start(bf16[8,48,2048]{2,1,0:T(8,128)(2,1)} %bitcast.1), calls=%async_computation | async-start | bytes 3145728 | tf_op jit(solution)/shard_map/all_to_all | solution.py:49
  162.8 158.2 %reduce-scatter.8.cloned.1.call-start = ((), (), s32[]{:S(2)}) async-start(), calls=%async_computation.12 | async-start | bytes 6127616 | tf_op jit(solution)/shard_map/reduce_scatter | solution.py:118
  199.2 1.1 copy-start.6
  205.4 1.2 copy-start.8
  205.4 162.4 %reduce-scatter.4.cloned.1.call-start = ((), (), s32[]{:S(2)}) async-start(), calls=%async_computation.10 | async-start | bytes 6127616 | tf_op jit(solution)/shard_map/reduce_scatter | solution.py:112
  211.8 1.2 copy-start.5
  211.8 238.6 %reduce-scatter.6.cloned.1.call-start = ((), (), s32[]{:S(2)}) async-start(), calls=%async_computation.11 | async-start | bytes 6127616 | tf_op jit(solution)/shard_map/reduce_scatter | solution.py:115
  218.2 4.9 %slice-start = ((s8[5767168]{0:T(1024)(128)(4,1)}), s8[1572864]{0:T(1024)(128)(4,1)S(1)}, s32[]{:S(2)}) async-start(s8[5767168]{0:T(1024)(128)(4,1)} %bitcast.108), calls=%async_computation.13 | async-start | bytes 3145728
  218.2 4.9 %slice-start.1 = ((s8[5767168]{0:T(1024)(128)(4,1)}), s8[4194304]{0:T(1024)(128)(4,1)S(1)}, s32[]{:S(2)}) async-start(s8[5767168]{0:T(1024)(128)(4,1)} %bitcast.108), calls=%async_computation.14 | async-start | bytes 8388608
  218.2 4.9 %copy-start.9 = (bf16[8,1,48,1408]{3,2,0,1:T(8,128)(2,1)S(1)}, bf16[8,1,48,1408]{3,2,0,1:T(8,128)(2,1)}, u32[]{:S(2)}) copy-start(bf16[8,1,48,1408]{3,2,0,1:T(8,128)(2,1)} %get-tuple-element.16) | copy-start | bytes 3244036
  226.9 4.5 copy-start.7
  226.9 26.1 %all-to-all-start.4 = ((bf16[8,48,2048]{2,1,0:T(8,128)(2,1)}), bf16[8,48,2048]{2,1,0:T(8,128)(2,1)S(1)}, u32[]{:S(2)}, u32[]{:S(2)}) async-start(bf16[8,48,2048]{2,1,0:T(8,128)(2,1)} %add_convert_fusion), calls=%async_computation.4 | async-start | bytes 3145728 | tf_op jit(solution)/shard_map/all_to_all | solution.py:97
  253.0 6.5 %copy-start.1 = (bf16[8,48,2048]{2,1,0:T(8,128)(2,1)}, bf16[8,48,2048]{2,1,0:T(8,128)(2,1)S(1)}, u32[]{:S(2)}) copy-start(bf16[8,48,2048]{2,1,0:T(8,128)(2,1)S(1)} %all-to-all-done.4) | copy-start | bytes 4718596
  253.0 36.1 %all-to-all-start.2 = ((bf16[8,48,2048]{2,1,0:T(8,128)(2,1)}), bf16[8,48,2048]{2,1,0:T(8,128)(2,1)S(1)}, u32[]{:S(2)}, u32[]{:S(2)}) async-start(bf16[8,48,2048]{2,1,0:T(8,128)(2,1)} %convolution_convert_fusion), calls=%async_computation.2 | async-start | bytes 3145728 | tf_op jit(solution)/shard_map/all_to_all | solution.py:63
  256.6 2.9 copy-start.4
  296.3 12.0 %copy-start = (f32[256,2048]{1,0:T(8,128)S(1)}, f32[256,2048]{1,0:T(8,128)}, u32[]{:S(2)}) copy-start(f32[256,2048]{1,0:T(8,128)} %convert_element_type.110) | copy-start | bytes 6291460
Sparse Core Ops, SparseCore 0:
  10.1 88.6 all-gather.4
  101.0 90.2 all-gather.2
  205.6 79.5 reduce-scatter.7
  288.4 79.3 reduce-scatter.3
  371.0 79.2 reduce-scatter.5
